TPU v7x, 128 devices: a whole 4x4x4 slice. The times are simulated.
128 devices in a mesh: seq: 32 (over z, x, core), batch: 4 (over y).
Axes of the slice: x: 4, y: 4, z: 4, core: 2. Of those that a mesh axis runs over, the one named last changes fastest.
Arguments:
- sequence_input: bfloat16 [32768, 1536], P(('batch', 'seq')), parts along dimension 0, may hold values from -6 to 6
- conv_first: bfloat16 [5, 1536, 768], replicated, may hold values from -0.0625 to 0.0625
- conv_second: bfloat16 [5, 768, 768], replicated, may hold values from -0.09375 to 0.09375
- qkv_weight: bfloat16 [768, 1536], replicated, may hold values from -0.21875 to 0.21875
- out_weight: bfloat16 [512, 768], replicated, may hold values from -0.25 to 0.25
- logit_scale: float32 [4], replicated, may hold values from 2.5 to 30, as said below
Outputs:
- block_output: bfloat16 [32768, 768], P(('batch', 'seq')), parts along dimension 0
There are 4 independent parts, one for each index of `batch`. A program takes and returns all parts, laid end to end along the dimension named above; an argument that names none is the same for every part. Nothing has to cross between parts.
Inputs may be any that keep to these rules, and one draw needn't show every extreme that they name: `logit_scale`: one positive scale a head.
All inputs are finite; a program needn't handle non-finite values.
Results may differ from a plain program's by a relative error of at most 0.023.
Values may be sent and summed in bfloat16 or wider, within the bound.
A program may use at most 256 MiB of HBM per device.

v0:
```python
import math
import jax
import jax.numpy as jnp
from jax import lax
from jax.sharding import PartitionSpec as P


def padded_2(block, sides, width):
    for axis, dim in sides:
        count = lax.axis_size(axis)
        forward = [(i, i + 1) for i in range(count - 1)]
        backward = [(target, source) for source, target in forward]
        low = lax.ppermute(
            lax.slice_in_dim(block, block.shape[dim] - width, None, axis=dim), axis, forward
        )
        high = lax.ppermute(lax.slice_in_dim(block, 0, width, axis=dim), axis, backward)
        block = jnp.concatenate([low, block, high], axis=dim)
    return block


def convolve(padded, weight, row_count):
    conv_sum = jnp.dot(padded[0:row_count], weight[0], preferred_element_type=jnp.float32)
    for offset in range(1, weight.shape[0]):
        conv_sum = conv_sum + jnp.dot(
            padded[offset : offset + row_count], weight[offset], preferred_element_type=jnp.float32
        )
    return conv_sum


def head_rms(tensor):
    return tensor * lax.rsqrt(jnp.mean(tensor * tensor, axis=-1, keepdims=True) + 1e-06)


def attend_block(state_now, queries, key_block, value_block):
    running_max, running_sum, running_out = state_now
    scores = jnp.einsum("thd,shd->hts", queries, key_block, preferred_element_type=jnp.float32)
    new_max = jnp.maximum(running_max, jnp.max(scores, axis=2))
    weights = jnp.exp(scores - new_max[:, :, None])
    running_sum = jnp.sum(weights, axis=2)
    running_out = jnp.einsum(
        "hts,shd->htd",
        weights.astype(jnp.bfloat16),
        value_block,
        preferred_element_type=jnp.float32,
    )
    return (new_max, running_sum, running_out)


def body(sequence_input, conv_first, conv_second, qkv_weight, out_weight, logit_scale):
    row_count = sequence_input.shape[0]
    padded_input = padded_2(sequence_input, (("seq", 0),), 2)
    first_out = jax.nn.gelu(convolve(padded_input, conv_first, row_count)).astype(jnp.bfloat16)
    padded_first = padded_2(first_out, (("seq", 0),), 2)
    second = convolve(padded_first, conv_second, row_count)
    hidden = (first_out.astype(jnp.float32) + second).astype(jnp.bfloat16)
    head_count = logit_scale.shape[0]
    width_all = qkv_weight.shape[1] // 3
    head_size = width_all // head_count
    query_part = jnp.dot(hidden, qkv_weight[:, :width_all], preferred_element_type=jnp.float32)
    query_part = query_part.reshape(row_count, head_count, head_size)
    queries = (head_rms(query_part) * (logit_scale / math.sqrt(head_size))[None, :, None]).astype(
        jnp.bfloat16
    )
    kv_weight = qkv_weight[:, width_all:]
    start_state = (
        jnp.full((head_count, row_count), -1e30, jnp.float32),
        jnp.zeros((head_count, row_count), jnp.float32),
        jnp.zeros((head_count, row_count, head_size), jnp.float32),
    )
    piece_rows = hidden.shape[0]
    paired = jnp.dot(hidden, kv_weight, preferred_element_type=jnp.float32)
    key_block = head_rms(paired[:, :width_all].reshape(piece_rows, head_count, head_size)).astype(
        jnp.bfloat16
    )
    value_block = (
        paired[:, width_all:].reshape(piece_rows, head_count, head_size).astype(jnp.bfloat16)
    )
    own_keys = key_block
    own_values = value_block
    flat_keys = own_keys.reshape(row_count, width_all)
    flat_values = own_values.reshape(row_count, width_all)
    piece_pair = (
        lax.all_gather(flat_keys, "seq", axis=0, tiled=True),
        lax.all_gather(flat_values, "seq", axis=0, tiled=True),
    )
    piece_rows = piece_pair[0].shape[0]
    key_block = piece_pair[0].reshape(piece_rows, head_count, head_size)
    value_block = piece_pair[1].reshape(piece_rows, head_count, head_size)
    final_state = attend_block(start_state, queries, key_block, value_block)
    running_max, running_sum, running_out = final_state
    attended = (
        (running_out / running_sum[:, :, None])
        .transpose(1, 0, 2)
        .reshape(row_count, width_all)
        .astype(jnp.bfloat16)
    )
    return (
        hidden.astype(jnp.float32)
        + jnp.dot(attended, out_weight, preferred_element_type=jnp.float32)
    ).astype(jnp.bfloat16)


def solution(mesh):
    in_specs = (P(("batch", "seq"), None), P(), P(), P(), P(), P())
    out_specs = P(("batch", "seq"), None)
    return jax.shard_map(body, mesh=mesh, in_specs=in_specs, out_specs=out_specs, check_vma=False)
```

profile of v0, /device:TPU:1, one launch (start us, length us, event | category | flops | bytes accessed | tf_op | source)
XLA Modules:
  0.0 185.4 jit_solution(1731052009252895028)
XLA Ops:
  6.5 0.8 fusion.101
  7.4 3.3 %collective-permute-start.1 = (bf16[2,1536]{1,0:T(2,128)(2,1)S(1)}, bf16[2,1536]{1,0:T(2,128)(2,1)S(1)}, u32[]{:S(2)}, u32[]{:S(2)}) collective-permute-start(bf16[2,1536]{1,0:T(2,128)(2,1)S(1)} %get-tuple-element.6), channel_id=1, source_target_pairs={{4,0},{8,4},{12,8},{16,12},{20,16},{24,20},{28,24},{32,28},{36,32}... | collective-permute-start | bytes 18440 | tf_op jit(solution)/shard_map/ppermute | solution.py:16
  10.7 3.5 %collective-permute-start = (bf16[2,1536]{1,0:T(2,128)(2,1)S(1)}, bf16[2,1536]{1,0:T(2,128)(2,1)S(1)}, u32[]{:S(2)}, u32[]{:S(2)}) collective-permute-start(bf16[2,1536]{1,0:T(2,128)(2,1)S(1)} %get-tuple-element.5), channel_id=1, source_target_pairs={{0,4},{4,8},{8,12},{12,16},{16,20},{20,24},{24,28},{28,32},{32,36}... | collective-permute-start | bytes 18440 | tf_op jit(solution)/shard_map/ppermute | solution.py:13
  14.2 2.7 %fusion.12 = f32[256,768]{1,0:T(8,128)S(1)} fusion(bf16[256,1536]{1,0:T(8,128)(2,1)} %param.6, bf16[5,1536,768]{2,1,0:T(8,128)(2,1)} %param.7), kind=kOutput, calls=%fused_computation.12 | convolution fusion | flops 603979776 | bytes 3932160 | tf_op jit(solution)/shard_map/dot_general | solution.py:24
  16.9 1.2 constant_dynamic-update-slice_fusion.1
  18.2 2.5 %fusion.8 = f32[256,768]{1,0:T(8,128)S(1)} fusion(bf16[5,1536,768]{2,1,0:T(8,128)(2,1)} %param.7, bf16[258,1536]{1,0:T(8,128)(2,1)S(1)} %constant_dynamic-update-slice_fusion), kind=kOutput, calls=%fused_computation.8 | convolution fusion | flops 603979776 | bytes 3932160 | tf_op jit(solution)/shard_map/dot_general | solution.py:24
  20.7 0.8 fusion.10
  21.5 0.8 fusion.14
  22.4 1.0 fusion.77
  23.4 2.9 %collective-permute-start.2 = (bf16[2,768]{1,0:T(2,128)(2,1)S(1)}, bf16[2,768]{1,0:T(2,128)(2,1)S(1)}, u32[]{:S(2)}, u32[]{:S(2)}) collective-permute-start(bf16[2,768]{1,0:T(2,128)(2,1)S(1)} %get-tuple-element.7), channel_id=1, source_target_pairs={{0,4},{4,8},{8,12},{12,16},{16,20},{20,24},{24,28},{28,32},{32,36}... | collective-permute-start | bytes 9224 | tf_op jit(solution)/shard_map/ppermute | solution.py:13
  26.4 0.5 fusion.54
  26.8 1.9 %collective-permute-start.3 = (bf16[2,768]{1,0:T(2,128)(2,1)S(1)}, bf16[2,768]{1,0:T(2,128)(2,1)S(1)}, u32[]{:S(2)}, u32[]{:S(2)}) collective-permute-start(bf16[2,768]{1,0:T(2,128)(2,1)S(1)} %get-tuple-element.8), channel_id=1, source_target_pairs={{4,0},{8,4},{12,8},{16,12},{20,16},{24,20},{28,24},{32,28},{36,32}... | collective-permute-start | bytes 9224 | tf_op jit(solution)/shard_map/ppermute | solution.py:16
  28.8 0.5 fusion.56
  29.3 2.5 %collective-permute-done.3 = bf16[2,768]{1,0:T(2,128)(2,1)S(1)} collective-permute-done((bf16[2,768]{1,0:T(2,128)(2,1)S(1)}, bf16[2,768]{1,0:T(2,128)(2,1)S(1)}, u32[]{:S(2)}, u32[]{:S(2)}) %collective-permute-start.3) | collective-permute-done | bytes 3104 | tf_op jit(solution)/shard_map/ppermute | solution.py:16
  31.8 0.5 fusion.51
  32.2 0.5 fusion.33
  32.8 0.5 fusion.40
  33.3 0.6 fusion.23
  34.1 0.3 reduce_sum.28
  34.5 0.3 mul.71
  34.9 0.8 fusion.87
  35.9 0.7 slice.220
  36.7 1.5 fusion.85
  38.4 0.3 multiply_reduce_fusion
  38.8 0.3 multiply_convert_fusion
  39.1 55.5 %all-gather.3.cloned.1.call-done = bf16[8192,512]{1,0:T(8,128)(2,1)} async-done(((bf16[256,512]{1,0:T(8,128)(2,1)}), bf16[8192,512]{1,0:T(8,128)(2,1)}) %all-gather.3.cloned.1.call-update) | async-done | bytes 8388624 | tf_op jit(solution)/shard_map/all_gather | solution.py:83
  94.6 16.8 %fusion.103 = (f32[4,256]{1,0:T(4,128)S(1)}, f32[4,256,8192]{2,1,0:T(8,128)}) fusion(bf16[256,4,128]{2,1,0:T(4,128)(2,1)S(1)} %multiply_convert_fusion, bf16[8192,512]{1,0:T(8,128)(2,1)} %all-gather.3.cloned.1.call-done), kind=kOutput, calls=%fused_computation.102 | convolution fusion | flops 2155871232 | bytes 42209280 | tf_op jit(solution)/shard_map/thd,shd->hts/dot_general | solution.py:36
  111.4 13.7 %fusion = f32[4,256]{1,0:T(4,128)S(1)} fusion(f32[4,256,8192]{2,1,0:T(8,128)} %get-tuple-element.10, f32[4,256]{1,0:T(4,128)S(1)} %broadcast_maximum_fusion), kind=kLoop, calls=%fused_computation.1 | loop fusion | flops 16776192 | bytes 33562624 | tf_op jit(solution)/shard_map/reduce_sum | solution.py:39
  125.2 24.3 %all-gather.5.cloned.1.call-done = bf16[8192,512]{1,0:T(8,128)(2,1)} async-done(((bf16[256,512]{1,0:T(8,128)(2,1)}), bf16[8192,512]{1,0:T(8,128)(2,1)}) %all-gather.5.cloned.1.call-update) | async-done | bytes 8388624 | tf_op jit(solution)/shard_map/all_gather | solution.py:84
  149.4 12.0 %copy.21 = bf16[8192,512]{0,1:T(8,128)(2,1)} copy(bf16[8192,512]{1,0:T(8,128)(2,1)} %all-gather.5.cloned.1.call-done) | data formatting | bytes 16777216 | tf_op jit(solution)/shard_map/reshape | solution.py:88
  161.4 16.0 %fusion.48 = bf16[256,4,128]{0,2,1:T(8,128)(2,1)S(1)} fusion(bf16[8192,4,128]{0,2,1:T(8,128)(2,1)} %bitcast.72, f32[4,256,8192]{2,1,0:T(8,128)} %get-tuple-element.10, f32[4,256]{1,0:T(4,128)S(1)} %broadcast_maximum_fusion, f32[256,4]{0,1:T(4,128)S(1)} %bitcast.77), kind=kOutput, calls=%fused_computation.39 | convolution fusion | flops 2164523008 | bytes 42213376 | tf_op jit(solution)/shard_map/hts,shd->htd/dot_general | solution.py:40
  177.5 1.1 fusion.41
  (31 shorter events, 0.8 us)
Async XLA Ops:
  6.5 170.9 %copy-start = (bf16[512,768]{1,0:T(8,128)(2,1)S(1)}, bf16[512,768]{1,0:T(8,128)(2,1)}, u32[]{:S(2)}) copy-start(bf16[512,768]{1,0:T(8,128)(2,1)} %param.10) | copy-start | bytes 2359300
  6.5 88.1 %all-gather.3.cloned.1.call-start = ((), (), s32[]{:S(2)}) async-start(), calls=%async_computation | async-start | bytes 8650752 | tf_op jit(solution)/shard_map/all_gather | solution.py:83
  7.4 10.8 %collective-permute-start.1 = (bf16[2,1536]{1,0:T(2,128)(2,1)S(1)}, bf16[2,1536]{1,0:T(2,128)(2,1)S(1)}, u32[]{:S(2)}, u32[]{:S(2)}) collective-permute-start(bf16[2,1536]{1,0:T(2,128)(2,1)S(1)} %get-tuple-element.6), channel_id=1, source_target_pairs={{4,0},{8,4},{12,8},{16,12},{20,16},{24,20},{28,24},{32,28},{36,32}... | collective-permute-start | bytes 18440 | tf_op jit(solution)/shard_map/ppermute | solution.py:16
  10.7 10.0 %copy-start.3 = (bf16[5,1536,768]{2,1,0:T(8,128)(2,1)S(1)}, bf16[5,1536,768]{2,1,0:T(8,128)(2,1)}, u32[]{:S(2)}) copy-start(bf16[5,1536,768]{2,1,0:T(8,128)(2,1)} %param.7) | copy-start | bytes 35389444
  10.7 10.8 %collective-permute-start = (bf16[2,1536]{1,0:T(2,128)(2,1)S(1)}, bf16[2,1536]{1,0:T(2,128)(2,1)S(1)}, u32[]{:S(2)}, u32[]{:S(2)}) collective-permute-start(bf16[2,1536]{1,0:T(2,128)(2,1)S(1)} %get-tuple-element.5), channel_id=1, source_target_pairs={{0,4},{4,8},{8,12},{12,16},{16,20},{20,24},{24,28},{28,32},{32,36}... | collective-permute-start | bytes 18440 | tf_op jit(solution)/shard_map/ppermute | solution.py:13
  18.1 3.4 %copy-start.2 = (bf16[256,1536]{1,0:T(8,128)(2,1)S(1)}, bf16[256,1536]{1,0:T(8,128)(2,1)}, u32[]{:S(2)}) copy-start(bf16[256,1536]{1,0:T(8,128)(2,1)} %param.6) | copy-start | bytes 2359300
  21.5 4.8 %slice-start = ((s8[5898240]{0:T(1024)(128)(4,1)}), s8[4194304]{0:T(1024)(128)(4,1)S(1)}, s32[]{:S(2)}) async-start(s8[5898240]{0:T(1024)(128)(4,1)} %bitcast.73), calls=%async_computation.2 | async-start | bytes 8388608
  22.4 4.0 %slice-start.1 = ((s8[5898240]{0:T(1024)(128)(4,1)}), s8[1703936]{0:T(1024)(128)(4,1)S(1)}, s32[]{:S(2)}) async-start(s8[5898240]{0:T(1024)(128)(4,1)} %bitcast.73), calls=%async_computation.3 | async-start | bytes 3407872
  23.4 5.4 %collective-permute-start.2 = (bf16[2,768]{1,0:T(2,128)(2,1)S(1)}, bf16[2,768]{1,0:T(2,128)(2,1)S(1)}, u32[]{:S(2)}, u32[]{:S(2)}) collective-permute-start(bf16[2,768]{1,0:T(2,128)(2,1)S(1)} %get-tuple-element.7), channel_id=1, source_target_pairs={{0,4},{4,8},{8,12},{12,16},{16,20},{20,24},{24,28},{28,32},{32,36}... | collective-permute-start | bytes 9224 | tf_op jit(solution)/shard_map/ppermute | solution.py:13
  26.8 4.9 %collective-permute-start.3 = (bf16[2,768]{1,0:T(2,128)(2,1)S(1)}, bf16[2,768]{1,0:T(2,128)(2,1)S(1)}, u32[]{:S(2)}, u32[]{:S(2)}) collective-permute-start(bf16[2,768]{1,0:T(2,128)(2,1)S(1)} %get-tuple-element.8), channel_id=1, source_target_pairs={{4,0},{8,4},{12,8},{16,12},{20,16},{24,20},{28,24},{32,28},{36,32}... | collective-permute-start | bytes 9224 | tf_op jit(solution)/shard_map/ppermute | solution.py:16
  29.3 4.0 %copy-start.1 = (bf16[768,1536]{1,0:T(8,128)(2,1)S(1)}, bf16[768,1536]{1,0:T(8,128)(2,1)}, u32[]{:S(2)}) copy-start(bf16[768,1536]{1,0:T(8,128)(2,1)} %param.9) | copy-start | bytes 7077892
  32.8 3.9 %copy-start.4 = (f32[4]{0:T(128)S(1)}, f32[4]{0:T(128)}, u32[]{:S(2)}) copy-start(f32[4]{0:T(128)} %param.11) | copy-start | bytes 52
  35.7 113.8 %all-gather.5.cloned.1.call-start = ((), (), s32[]{:S(2)}) async-start(), calls=%async_computation.1 | async-start | bytes 8650752 | tf_op jit(solution)/shard_map/all_gather | solution.py:84
Sparse Core Ops, SparseCore 0:
  35.8 58.7 all-gather.2
  96.9 52.5 all-gather.4
where the time goes:
time: 186 us; the launch traced here: 185 us
  waiting for transfers between devices  82.3 us (44%)
  matrix products  46.4 us (25%)
  other arithmetic  15.6 us (8%)
  local copies, waits for them, and re-layouts  15.5 us (8%)
  between operations  13.8 us (7%)
  starting transfers between devices  11.9 us (6%)
    all_gather x1, waiting for transfers between devices, body(): lax.all_gather(flat_keys, 'seq', axis=0, tiled=True)  55.5 us
    all_gather x1, waiting for transfers between devices, body(): lax.all_gather(flat_values, 'seq', axis=0, tiled=True)  24.3 us
    dot_general x1, matrix products, attend_block(): jnp.einsum('thd,shd->hts', queries, key_block, preferred_element_type=jnp...  16.8 us
    dot_general x1, matrix products, attend_block(): jnp.einsum('hts,shd->htd', weights.astype(jnp.bfloat16), value_block, pre...  16 us
    reduce_sum x1, other arithmetic, attend_block(): running_sum = jnp.sum(weights, axis=2)  13.7 us
    reshape x1, local copies, waits for them, and re-layouts, body(): value_block = piece_pair[1].reshape(piece_rows, head_count, head_size)  12 us
    dot_general x8, matrix products, convolve(): jnp.dot(padded[offset:offset + row_count], weight[offset], preferred_elem...  8.8 us
    ppermute x2, starting transfers between devices, padded_2(): lax.ppermute(lax.slice_in_dim(block, block.shape[dim] - width, None, axis...  6.42 us
  transfers between devices with their start and end apart: 6, of which 3 were waited for; matrix products, arithmetic and copies ran while one was open for 23% of the time, Pallas kernels for 0%

commit v1 on v0

--- a/solution.py
+++ b/solution.py
@@ -3,6 +3,14 @@
 import jax.numpy as jnp
 from jax import lax
 from jax.sharding import PartitionSpec as P
+
+
+def tiled_gather(array, axis, dim):
+    size = lax.axis_size(axis)
+    repeats = [size if d == dim else 1 for d in range(array.ndim)]
+    return lax.all_to_all(
+        jnp.tile(array, repeats), axis, split_axis=dim, concat_axis=dim, tiled=True
+    )
 
 
 def padded_2(block, sides, width):
@@ -80,7 +88,7 @@
     flat_keys = own_keys.reshape(row_count, width_all)
     flat_values = own_values.reshape(row_count, width_all)
     piece_pair = (
-        lax.all_gather(flat_keys, "seq", axis=0, tiled=True),
+        tiled_gather(flat_keys, "seq", 0),
         lax.all_gather(flat_values, "seq", axis=0, tiled=True),
     )
     piece_rows = piece_pair[0].shape[0]

time: 186 us -> 263 us (1.41)
  the two profiles are of different devices: /device:TPU:1 before, /device:TPU:0 now
where the time goes in v1:
time: 263 us; the launch traced here: 262 us
  waiting for transfers between devices  120 us (46%)
  matrix products  46.1 us (18%)
  local copies, waits for them, and re-layouts  44.7 us (17%)
  starting transfers between devices  23.2 us (9%)
  other arithmetic  14.9 us (6%)
  between operations  13.8 us (5%)
    all_to_all x1, waiting for transfers between devices, tiled_gather(): lax.all_to_all(jnp.tile(array, repeats), axis, split_axis=dim, concat_axi...  118 us
    dot_general x1, matrix products, attend_block(): jnp.einsum('thd,shd->hts', queries, key_block, preferred_element_type=jnp...  16.5 us
    dot_general x1, matrix products, attend_block(): jnp.einsum('hts,shd->htd', weights.astype(jnp.bfloat16), value_block, pre...  16 us
    all_to_all x1, starting transfers between devices, tiled_gather(): lax.all_to_all(jnp.tile(array, repeats), axis, split_axis=dim, concat_axi...  14.1 us
    reduce_sum x1, other arithmetic, attend_block(): running_sum = jnp.sum(weights, axis=2)  13.6 us
    reshape x1, local copies, waits for them, and re-layouts, body(): key_block = piece_pair[0].reshape(piece_rows, head_count, head_size)  13.4 us
    reshape x1, local copies, waits for them, and re-layouts, body(): value_block = piece_pair[1].reshape(piece_rows, head_count, head_size)  12 us
    all_to_all x1, local copies, waits for them, and re-layouts, tiled_gather(): lax.all_to_all(jnp.tile(array, repeats), axis, split_axis=dim, concat_axi...  11.4 us
  transfers between devices with their start and end apart: 6, of which 2 were waited for; matrix products, arithmetic and copies ran while one was open for 27% of the time, Pallas kernels for 0%

profile of v1, /device:TPU:0, one launch (start us, length us, event | category | flops | bytes accessed | tf_op | source)
XLA Modules:
  0.0 262.2 jit_solution(4857593313068001192)
XLA Ops:
  6.5 0.8 fusion.99
  7.4 1.3 collective-permute-start.1
  8.7 3.4 %collective-permute-start = (bf16[2,1536]{1,0:T(2,128)(2,1)S(1)}, bf16[2,1536]{1,0:T(2,128)(2,1)S(1)}, u32[]{:S(2)}, u32[]{:S(2)}) collective-permute-start(bf16[2,1536]{1,0:T(2,128)(2,1)S(1)} %get-tuple-element.5), channel_id=1, source_target_pairs={{0,4},{4,8},{8,12},{12,16},{16,20},{20,24},{24,28},{28,32},{32,36}... | collective-permute-start | bytes 18440 | tf_op jit(solution)/shard_map/ppermute | solution.py:21
  12.1 2.7 %fusion.9 = f32[256,768]{1,0:T(8,128)S(1)} fusion(bf16[256,1536]{1,0:T(8,128)(2,1)} %param.6, bf16[5,1536,768]{2,1,0:T(8,128)(2,1)} %param.7), kind=kOutput, calls=%fused_computation.9 | convolution fusion | flops 603979776 | bytes 3932160 | tf_op jit(solution)/shard_map/dot_general | solution.py:32
  14.8 1.2 constant_dynamic-update-slice_fusion.1
  16.1 2.5 fusion.5
  18.6 0.8 fusion.7
  19.4 0.8 fusion.11
  20.3 1.0 fusion.74
  21.3 3.1 %collective-permute-start.2 = (bf16[2,768]{1,0:T(2,128)(2,1)S(1)}, bf16[2,768]{1,0:T(2,128)(2,1)S(1)}, u32[]{:S(2)}, u32[]{:S(2)}) collective-permute-start(bf16[2,768]{1,0:T(2,128)(2,1)S(1)} %get-tuple-element.7), channel_id=1, source_target_pairs={{0,4},{4,8},{8,12},{12,16},{16,20},{20,24},{24,28},{28,32},{32,36}... | collective-permute-start | bytes 9224 | tf_op jit(solution)/shard_map/ppermute | solution.py:21
  24.4 0.5 fusion.51
  24.9 1.3 collective-permute-start.3
  26.2 0.5 fusion.53
  26.7 1.8 collective-permute-done.3
  28.5 0.5 fusion.48
  29.0 0.5 fusion.30
  29.5 0.5 fusion.37
  30.0 0.6 fusion.20
  30.6 0.7 slice.220
  32.6 4.2 %tile.2 = bf16[32,256,512]{1,2,0:T(8,128)(2,1)} broadcast(bf16[256,512]{0,1:T(8,128)(2,1)S(1)} %copy.24), dimensions={1,2} | broadcast | bytes 8650752 | tf_op jit(solution)/shard_map/tile | solution.py:12
  36.7 14.1 %all-to-all-start = ((bf16[32,256,512]{1,2,0:T(8,128)(2,1)}), bf16[32,256,512]{1,2,0:T(8,128)(2,1)}, u32[]{:S(2)}, u32[]{:S(2)}) async-start(bf16[32,256,512]{1,2,0:T(8,128)(2,1)} %tile.2), calls=%async_computation | async-start | bytes 16777216 | tf_op jit(solution)/shard_map/all_to_all | solution.py:11
  50.8 1.5 fusion.82
  52.5 0.3 multiply_reduce_fusion
  52.9 0.3 multiply_convert_fusion
  53.3 117.9 %all-to-all-done = bf16[32,256,512]{1,2,0:T(8,128)(2,1)} async-done(((bf16[32,256,512]{1,2,0:T(8,128)(2,1)}), bf16[32,256,512]{1,2,0:T(8,128)(2,1)}, u32[]{:S(2)}, u32[]{:S(2)}) %all-to-all-start) | async-done | bytes 8388640 | tf_op jit(solution)/shard_map/all_to_all | solution.py:11
  171.1 11.4 %copy.25 = bf16[32,256,512]{1,0,2:T(8,128)(2,1)} copy(bf16[32,256,512]{1,2,0:T(8,128)(2,1)} %all-to-all-done) | data formatting | bytes 16777216 | tf_op jit(solution)/shard_map/all_to_all | solution.py:11
  182.5 13.4 %reshape.52 = bf16[8192,4,128]{0,2,1:T(8,128)(2,1)} reshape(bf16[32,256,512]{1,0,2:T(8,128)(2,1)} %copy.25) | data formatting | bytes 16777216 | tf_op jit(solution)/shard_map/reshape | solution.py:95
  196.0 16.5 %fusion.101 = (f32[4,256]{1,0:T(4,128)S(1)}, f32[4,256,8192]{2,1,0:T(8,128)}) fusion(bf16[8192,4,128]{0,2,1:T(8,128)(2,1)} %reshape.52, bf16[256,4,128]{2,1,0:T(4,128)(2,1)S(1)} %multiply_convert_fusion), kind=kOutput, calls=%fused_computation.100 | convolution fusion | flops 2155871232 | bytes 42209280 | tf_op jit(solution)/shard_map/thd,shd->hts/dot_general | solution.py:44
  212.5 13.6 %fusion = f32[4,256]{1,0:T(4,128)S(1)} fusion(f32[4,256,8192]{2,1,0:T(8,128)} %get-tuple-element.10, f32[4,256]{1,0:T(4,128)S(1)} %broadcast_maximum_fusion), kind=kLoop, calls=%fused_computation.1 | loop fusion | flops 16776192 | bytes 33562624 | tf_op jit(solution)/shard_map/reduce_sum | solution.py:47
  226.2 12.0 %copy.30 = bf16[8192,512]{0,1:T(8,128)(2,1)} copy(bf16[8192,512]{1,0:T(8,128)(2,1)} %all-gather.2.cloned.1.call-done) | data formatting | bytes 16777216 | tf_op jit(solution)/shard_map/reshape | solution.py:96
  238.2 16.0 %fusion.45 = bf16[256,4,128]{0,2,1:T(8,128)(2,1)S(1)} fusion(bf16[8192,4,128]{0,2,1:T(8,128)(2,1)} %bitcast.66, f32[4,256,8192]{2,1,0:T(8,128)} %get-tuple-element.10, f32[4,256]{1,0:T(4,128)S(1)} %broadcast_maximum_fusion, f32[256,4]{0,1:T(4,128)S(1)} %bitcast.71), kind=kOutput, calls=%fused_computation.36 | convolution fusion | flops 2164523008 | bytes 42213376 | tf_op jit(solution)/shard_map/hts,shd->htd/dot_general | solution.py:48
  254.3 1.1 fusion.38
  (34 shorter events, 1.5 us)
Async XLA Ops:
  6.5 247.7 %copy-start = (bf16[512,768]{1,0:T(8,128)(2,1)S(1)}, bf16[512,768]{1,0:T(8,128)(2,1)}, u32[]{:S(2)}) copy-start(bf16[512,768]{1,0:T(8,128)(2,1)} %param.10) | copy-start | bytes 2359300
  6.5 219.6 %all-gather.2.cloned.1.call-start = ((), (), s32[]{:S(2)}) async-start(), calls=%async_computation.1 | async-start | bytes 8650752 | tf_op jit(solution)/shard_map/all_gather | solution.py:92
  7.4 8.7 %collective-permute-start.1 = (bf16[2,1536]{1,0:T(2,128)(2,1)S(1)}, bf16[2,1536]{1,0:T(2,128)(2,1)S(1)}, u32[]{:S(2)}, u32[]{:S(2)}) collective-permute-start(bf16[2,1536]{1,0:T(2,128)(2,1)S(1)} %get-tuple-element.6), channel_id=1, source_target_pairs={{4,0},{8,4},{12,8},{16,12},{20,16},{24,20},{28,24},{32,28},{36,32}... | collective-permute-start | bytes 18440 | tf_op jit(solution)/shard_map/ppermute | solution.py:24
  8.7 9.9 %copy-start.3 = (bf16[5,1536,768]{2,1,0:T(8,128)(2,1)S(1)}, bf16[5,1536,768]{2,1,0:T(8,128)(2,1)}, u32[]{:S(2)}) copy-start(bf16[5,1536,768]{2,1,0:T(8,128)(2,1)} %param.7) | copy-start | bytes 35389444
  8.7 10.7 %collective-permute-start = (bf16[2,1536]{1,0:T(2,128)(2,1)S(1)}, bf16[2,1536]{1,0:T(2,128)(2,1)S(1)}, u32[]{:S(2)}, u32[]{:S(2)}) collective-permute-start(bf16[2,1536]{1,0:T(2,128)(2,1)S(1)} %get-tuple-element.5), channel_id=1, source_target_pairs={{0,4},{4,8},{8,12},{12,16},{16,20},{20,24},{24,28},{28,32},{32,36}... | collective-permute-start | bytes 18440 | tf_op jit(solution)/shard_map/ppermute | solution.py:21
  16.0 3.4 %copy-start.2 = (bf16[256,1536]{1,0:T(8,128)(2,1)S(1)}, bf16[256,1536]{1,0:T(8,128)(2,1)}, u32[]{:S(2)}) copy-start(bf16[256,1536]{1,0:T(8,128)(2,1)} %param.6) | copy-start | bytes 2359300
  19.4 5.0 %slice-start = ((s8[5898240]{0:T(1024)(128)(4,1)}), s8[4194304]{0:T(1024)(128)(4,1)S(1)}, s32[]{:S(2)}) async-start(s8[5898240]{0:T(1024)(128)(4,1)} %bitcast.67), calls=%async_computation.2 | async-start | bytes 8388608
  20.2 4.2 %slice-start.1 = ((s8[5898240]{0:T(1024)(128)(4,1)}), s8[1703936]{0:T(1024)(128)(4,1)S(1)}, s32[]{:S(2)}) async-start(s8[5898240]{0:T(1024)(128)(4,1)} %bitcast.67), calls=%async_computation.3 | async-start | bytes 3407872
  21.3 4.9 %collective-permute-start.2 = (bf16[2,768]{1,0:T(2,128)(2,1)S(1)}, bf16[2,768]{1,0:T(2,128)(2,1)S(1)}, u32[]{:S(2)}, u32[]{:S(2)}) collective-permute-start(bf16[2,768]{1,0:T(2,128)(2,1)S(1)} %get-tuple-element.7), channel_id=1, source_target_pairs={{0,4},{4,8},{8,12},{12,16},{16,20},{20,24},{24,28},{28,32},{32,36}... | collective-permute-start | bytes 9224 | tf_op jit(solution)/shard_map/ppermute | solution.py:21
  24.9 3.6 %collective-permute-start.3 = (bf16[2,768]{1,0:T(2,128)(2,1)S(1)}, bf16[2,768]{1,0:T(2,128)(2,1)S(1)}, u32[]{:S(2)}, u32[]{:S(2)}) collective-permute-start(bf16[2,768]{1,0:T(2,128)(2,1)S(1)} %get-tuple-element.8), channel_id=1, source_target_pairs={{4,0},{8,4},{12,8},{16,12},{20,16},{24,20},{28,24},{32,28},{36,32}... | collective-permute-start | bytes 9224 | tf_op jit(solution)/shard_map/ppermute | solution.py:24
  26.7 3.3 %copy-start.1 = (bf16[768,1536]{1,0:T(8,128)(2,1)S(1)}, bf16[768,1536]{1,0:T(8,128)(2,1)}, u32[]{:S(2)}) copy-start(bf16[768,1536]{1,0:T(8,128)(2,1)} %param.9) | copy-start | bytes 7077892
  36.7 14.1 %copy-start.4 = (f32[4]{0:T(128)S(1)}, f32[4]{0:T(128)}, u32[]{:S(2)}) copy-start(f32[4]{0:T(128)} %param.11) | copy-start | bytes 52
  36.7 134.4 %all-to-all-start = ((bf16[32,256,512]{1,2,0:T(8,128)(2,1)}), bf16[32,256,512]{1,2,0:T(8,128)(2,1)}, u32[]{:S(2)}, u32[]{:S(2)}) async-start(bf16[32,256,512]{1,2,0:T(8,128)(2,1)} %tile.2), calls=%async_computation | async-start | bytes 16777216 | tf_op jit(solution)/shard_map/all_to_all | solution.py:11
Sparse Core Ops, SparseCore 0:
  31.5 135.2 all-gather.1
